TPU v7x, 32 devices: a whole 2x2x4 slice. The times are simulated.
32 devices in a mesh: branch: 2 (over core), seq: 4 (over z), head: 4 (over y, x).
Axes of the slice: x: 2, y: 2, z: 4, core: 2. Of those that a mesh axis runs over, the one named last changes fastest.
Arguments:
- tokens: bfloat16 [1024, 3072], P('seq', 'head'), may hold values from -10 to 10
- valid_counts: int32 [4], P('seq'), may hold values from 1 to 256, 768 in all
- shared_qkv: bfloat16 [3072, 3, 1536], P('branch', None, 'head'), may hold values from -0.08479832 to 0.08479832
- shared_out: bfloat16 [1536, 3072], P('head', 'branch'), may hold values from -0.15625 to 0.15625
- skipped_qkv: bfloat16 [3072, 3, 1536], P('branch', None, 'head'), may hold values from -0.08479832 to 0.08479832
- skipped_out: bfloat16 [1536, 3072], P('head', 'branch'), may hold values from -0.15625 to 0.15625
- modulation: float32 [2, 3, 3072], replicated, may hold values from -3 to 3
- qk_gains: float32 [2, 2, 128], replicated, may hold values from 1.2 to 5.5
Outputs:
- branches: bfloat16 [2, 1024, 3072], P('branch', 'seq', 'head')
Inputs may be any that keep to these rules, and one draw needn't show every extreme that they name: `valid_counts`: each entry counts the leading real tokens of one shard of 256 slots; the rest are padding. The entries sum to 768 and one of them equals 256.
All inputs are finite; a program needn't handle non-finite values.
Results may differ from a plain program's by a relative error of at most 0.01.
Values may be sent and summed in bfloat16 or wider, within the bound.
No kernel may reach another device: no remote copies, remote signals or barrier semaphores. Data moves between devices by JAX's collectives and lax.ppermute only.
A program may use at most 128 MiB of HBM per device.

v0:
```python
import jax
import jax.numpy as jnp
from jax import lax
from jax.sharding import PartitionSpec as P

HEAD_DIM = 128


def modulate(x_rows, mod):
    whole = lax.all_gather(x_rows, "head", axis=1, tiled=True)
    xf = whole.astype(jnp.float32)
    mean = jnp.mean(xf, axis=1, keepdims=True)
    centered = xf - mean
    var = jnp.mean(centered * centered, axis=1, keepdims=True)
    normed = centered * lax.rsqrt(var + 1e-06)
    return (normed * (1.0 + mod[1]) + mod[0]).astype(jnp.bfloat16)


def attend_block(x_full, keep_full, qkv_weight, out_weight, mod, gains):
    rows, quarter = x_full.shape
    width = qkv_weight.shape[2]
    group = width // HEAD_DIM
    moded = modulate(x_full, mod)
    qkv = jnp.einsum(
        "rd,dsc->rsc",
        moded,
        lax.all_gather(qkv_weight, "branch", axis=0, tiled=True),
        preferred_element_type=jnp.float32,
    )
    qpart = qkv[:, 0].reshape(rows, group, HEAD_DIM)
    kpart = qkv[:, 1].reshape(rows, group, HEAD_DIM)
    query = (
        qpart * lax.rsqrt(jnp.mean(qpart * qpart, axis=2, keepdims=True) + 1e-06) * gains[0]
    ).astype(jnp.bfloat16)
    key = (
        kpart * lax.rsqrt(jnp.mean(kpart * kpart, axis=2, keepdims=True) + 1e-06) * gains[1]
    ).astype(jnp.bfloat16)
    key = key.reshape(rows, width)
    value = qkv[:, 2].astype(jnp.bfloat16)
    scale = 1.0 / HEAD_DIM**0.5
    keep_wire = keep_full.astype(jnp.bfloat16)
    peak = jnp.full((group, rows), -1e30, jnp.float32)
    key_piece = lax.all_gather(key, "seq", axis=0, tiled=True)
    value_piece = lax.all_gather(value, "seq", axis=0, tiled=True)
    keep_piece = lax.all_gather(keep_wire, "seq", axis=0, tiled=True)
    length = key_piece.shape[0]
    key_heads = key_piece.reshape(length, group, HEAD_DIM)
    value_heads = value_piece.reshape(length, group, HEAD_DIM)
    scores = (
        jnp.einsum("rhd,nhd->hrn", query, key_heads, preferred_element_type=jnp.float32) * scale
    )
    valid = keep_piece[None, None, :] > 0.5
    scores = jnp.where(valid, scores, -1e30)
    new_peak = jnp.maximum(peak, jnp.max(scores, axis=2))
    weights = jnp.where(valid, jnp.exp(scores - new_peak[:, :, None]), 0.0)
    total = jnp.sum(weights, axis=2)
    mixed = jnp.einsum(
        "hrn,nhd->hrd",
        weights.astype(jnp.bfloat16),
        value_heads,
        preferred_element_type=jnp.float32,
    )
    attended = (mixed / total[:, :, None]).astype(jnp.bfloat16)
    attended = attended.transpose(1, 0, 2).reshape(rows, width)
    projected = jnp.dot(
        attended,
        lax.all_gather(out_weight, "branch", axis=1, tiled=True),
        preferred_element_type=jnp.float32,
    )
    mine = lax.psum_scatter(projected, "head", scatter_dimension=1, tiled=True)
    gate = lax.dynamic_slice_in_dim(mod[2], lax.axis_index("head") * quarter, quarter, 0)
    return (x_full.astype(jnp.float32) + gate[None, :] * mine).astype(jnp.bfloat16)


def full_block(x_full, keep_full, qkv_weight, out_weight, mod, gains):
    updated = attend_block(x_full, keep_full, qkv_weight, out_weight, mod, gains)
    return updated


def per_device(
    tokens, valid_counts, shared_qkv, shared_out, skipped_qkv, skipped_out, modulation, qk_gains
):
    rows = tokens.shape[0]
    positions = jnp.arange(rows, dtype=jnp.int32)
    keep_all = (positions < valid_counts[0]).astype(jnp.float32)
    forked = full_block(tokens, keep_all, shared_qkv, shared_out, modulation[0], qk_gains[0])
    strong = full_block(forked, keep_all, skipped_qkv, skipped_out, modulation[1], qk_gains[1])
    result = jnp.where(lax.axis_index("branch") == 0, strong, forked)
    return result[None]


def solution(mesh):
    in_specs = (
        P("seq", "head"),
        P("seq"),
        P("branch", None, "head"),
        P("head", "branch"),
        P("branch", None, "head"),
        P("head", "branch"),
        P(),
        P(),
    )
    out_specs = P("branch", "seq", "head")
    return jax.shard_map(
        per_device, mesh=mesh, in_specs=in_specs, out_specs=out_specs, check_vma=False
    )
```

profile of v0, /device:TPU:0, one launch (start us, length us, event | category | flops | bytes accessed | tf_op | source)
XLA Modules:
  0.0 313.8 jit_solution(11347913517500845164)
XLA Ops:
  9.6 12.7 %all-gather.2 = bf16[4,1,256]{2,1,0:T(2,128)(2,1)S(1)} all-gather(bf16[1,1,256]{2,1,0:T(2,128)(2,1)S(1)} %reshape.146), channel_id=1, replica_groups=mesh['branch'=2,'seq'=4,'head'=4] {'seq'}, dimensions={0}, use_global_device_ids=true | all-gather | bytes 2560 | tf_op jit(solution)/shard_map/all_gather | solution.py:45
  22.3 20.5 %all-gather.10.cloned.1.call-done = bf16[256,3072]{1,0:T(8,128)(2,1)} async-done(((bf16[256,768]{1,0:T(8,128)(2,1)}), bf16[256,3072]{1,0:T(8,128)(2,1)}) %all-gather.10.cloned.1.call-update) | async-done | bytes 1572880 | tf_op jit(solution)/shard_map/all_gather | solution.py:10
  42.8 1.8 convert_reduce_fusion.1
  44.6 2.0 fusion.8
  46.6 15.7 %all-gather.12.cloned.1.call-done = bf16[3072,3,384]{2,0,1:T(8,128)(2,1)} async-done(((bf16[1536,3,384]{2,0,1:T(8,128)(2,1)}), bf16[3072,3,384]{2,0,1:T(8,128)(2,1)}) %all-gather.12.cloned.1.call-update) | async-done | bytes 7077904 | tf_op jit(solution)/shard_map/all_gather | solution.py:27
  62.3 5.3 %fusion.19 = f32[256,3,384]{2,0,1:T(8,128)S(1)} fusion(bf16[3072,3,384]{2,0,1:T(8,128)(2,1)} %all-gather.12.cloned.1.call-done, bf16[256,3072]{1,0:T(8,128)(2,1)S(1)} %copy-done, f32[3072]{0:T(1024)S(1)} %bitcast.90, f32[3072]{0:T(1024)S(1)} %bitcast.91, f32[256]{0:T(256)S(1)} %add_rsqrt_fusion.5, f32[256]{0:T(256)S(1)} %broadcast_multiply_fusion.1), kind=kOutput, calls=%fused_computation.27 | convolution fusion | flops 1816657920 | bytes 9857024 | tf_op jit(solution)/shard_map/rd,dsc->rsc/dot_general | solution.py:24
  68.1 19.8 %all_gather.37 = bf16[1024,384]{1,0:T(8,128)(2,1)S(1)} all-gather(bf16[256,384]{1,0:T(8,128)(2,1)S(1)} %fusion.61), channel_id=1, replica_groups=mesh['branch'=2,'seq'=4,'head'=4] {'seq'}, dimensions={0}, use_global_device_ids=true | all-gather | bytes 983040 | tf_op jit(solution)/shard_map/all_gather | solution.py:43
  88.4 18.0 %all-gather = bf16[1024,1,384]{2,0,1:T(8,128)(2,1)S(1)} all-gather(bf16[256,1,384]{2,0,1:T(8,128)(2,1)S(1)} %slice.109), channel_id=2, replica_groups=mesh['branch'=2,'seq'=4,'head'=4] {'seq'}, dimensions={0}, use_global_device_ids=true | all-gather | bytes 983040 | tf_op jit(solution)/shard_map/all_gather | solution.py:44
  108.5 0.9 fusion.53
  109.5 4.4 %fusion.78 = f32[256,3072]{1,0:T(8,128)} fusion(bf16[256,384]{0,1:T(8,128)(2,1)S(1)} %bitcast.87, bf16[384,3072]{1,0:T(8,128)(2,1)} %all-gather.14.cloned.1.call-done), kind=kOutput, calls=%fused_computation.104 | convolution fusion | flops 603979776 | bytes 5701632 | tf_op jit(solution)/shard_map/dot_general | solution.py:65
  114.0 43.3 %reduce-scatter.3.cloned.1.call-done = f32[256,768]{1,0:T(8,128)} async-done(((f32[256,3072]{1,0:T(8,128)}), f32[256,768]{1,0:T(8,128)}) %reduce-scatter.3.cloned.1.call-update) | async-done | bytes 786448 | tf_op jit(solution)/shard_map/reduce_scatter | solution.py:70
  157.3 2.0 add_convert_fusion.1
  160.7 29.6 %all-gather.16.cloned.1.call-done = bf16[256,3072]{1,0:T(8,128)(2,1)} async-done(((bf16[256,768]{1,0:T(8,128)(2,1)}), bf16[256,3072]{1,0:T(8,128)(2,1)}) %all-gather.16.cloned.1.call-update) | async-done | bytes 1572880 | tf_op jit(solution)/shard_map/all_gather | solution.py:10
  190.3 1.8 convert_reduce_fusion
  192.2 2.0 fusion.4
  194.1 15.5 %all-gather.18.cloned.1.call-done = bf16[3072,3,384]{2,0,1:T(8,128)(2,1)} async-done(((bf16[1536,3,384]{2,0,1:T(8,128)(2,1)}), bf16[3072,3,384]{2,0,1:T(8,128)(2,1)}) %all-gather.18.cloned.1.call-update) | async-done | bytes 7077904 | tf_op jit(solution)/shard_map/all_gather | solution.py:27
  209.7 5.3 %fusion.22 = f32[256,3,384]{2,0,1:T(8,128)S(1)} fusion(bf16[3072,3,384]{2,0,1:T(8,128)(2,1)} %all-gather.18.cloned.1.call-done, bf16[256,3072]{1,0:T(8,128)(2,1)S(1)} %copy-done.1, f32[3072]{0:T(1024)S(1)} %bitcast.88, f32[3072]{0:T(1024)S(1)} %bitcast.89, f32[256]{0:T(256)S(1)} %add_rsqrt_fusion.4, f32[256]{0:T(256)S(1)} %broadcast_multiply_fusion), kind=kOutput, calls=%fused_computation.29 | convolution fusion | flops 1816657920 | bytes 9857024 | tf_op jit(solution)/shard_map/rd,dsc->rsc/dot_general | solution.py:24
  215.5 19.8 %all_gather.42 = bf16[1024,384]{1,0:T(8,128)(2,1)S(1)} all-gather(bf16[256,384]{1,0:T(8,128)(2,1)S(1)} %fusion.59), channel_id=1, replica_groups=mesh['branch'=2,'seq'=4,'head'=4] {'seq'}, dimensions={0}, use_global_device_ids=true | all-gather | bytes 983040 | tf_op jit(solution)/shard_map/all_gather | solution.py:43
  235.8 18.2 %all-gather.1 = bf16[1024,1,384]{2,0,1:T(8,128)(2,1)S(1)} all-gather(bf16[256,1,384]{2,0,1:T(8,128)(2,1)S(1)} %slice.108), channel_id=3, replica_groups=mesh['branch'=2,'seq'=4,'head'=4] {'seq'}, dimensions={0}, use_global_device_ids=true | all-gather | bytes 983040 | tf_op jit(solution)/shard_map/all_gather | solution.py:44
  255.2 0.9 fusion.16
  256.1 0.9 fusion.47
  257.1 4.4 %fusion.79 = f32[256,3072]{1,0:T(8,128)} fusion(bf16[256,384]{0,1:T(8,128)(2,1)S(1)} %bitcast.86, bf16[384,3072]{1,0:T(8,128)(2,1)} %all-gather.20.cloned.1.call-done), kind=kOutput, calls=%fused_computation.105 | convolution fusion | flops 603979776 | bytes 5701632 | tf_op jit(solution)/shard_map/dot_general | solution.py:65
  261.5 43.4 %reduce-scatter.5.cloned.1.call-done = f32[256,768]{1,0:T(8,128)} async-done(((f32[256,3072]{1,0:T(8,128)}), f32[256,768]{1,0:T(8,128)}) %reduce-scatter.5.cloned.1.call-update) | async-done | bytes 786448 | tf_op jit(solution)/shard_map/reduce_scatter | solution.py:70
  304.9 2.0 fusion.57
  (75 shorter events, 9.1 us)
Async XLA Ops:
  6.5 2.3 copy-start.4
  6.5 2.3 copy-start.5
  6.5 36.2 %all-gather.10.cloned.1.call-start = ((), (), s32[]{:S(2)}) async-start(), calls=%async_computation.2 | async-start | bytes 1966080 | tf_op jit(solution)/shard_map/all_gather | solution.py:10
  7.3 55.0 %all-gather.12.cloned.1.call-start = ((), (), s32[]{:S(2)}) async-start(), calls=%async_computation.3 | async-start | bytes 10616832 | tf_op jit(solution)/shard_map/all_gather | solution.py:27
  8.0 101.5 %all-gather.14.cloned.1.call-start = ((), (), s32[]{:S(2)}) async-start(), calls=%async_computation.4 | async-start | bytes 3538944 | tf_op jit(solution)/shard_map/all_gather | solution.py:67
  8.7 148.6 %reduce-scatter.3.cloned.1.call-start = ((), (), s32[]{:S(2)}) async-start(), calls=%async_computation.5 | async-start | bytes 3932160 | tf_op jit(solution)/shard_map/reduce_scatter | solution.py:70
  42.8 19.5 %copy-start = (bf16[256,3072]{1,0:T(8,128)(2,1)S(1)}, bf16[256,3072]{1,0:T(8,128)(2,1)}, u32[]{:S(2)}) copy-start(bf16[256,3072]{1,0:T(8,128)(2,1)} %all-gather.10.cloned.1.call-done) | copy-start | bytes 4718596
  109.5 47.8 %copy-start.3 = (bf16[256,768]{1,0:T(8,128)(2,1)S(1)}, bf16[256,768]{1,0:T(8,128)(2,1)}, u32[]{:S(2)}) copy-start(bf16[256,768]{1,0:T(8,128)(2,1)} %param.8) | copy-start | bytes 1179652
  113.9 76.4 %all-gather.16.cloned.1.call-start = ((), (), s32[]{:S(2)}) async-start(), calls=%async_computation.6 | async-start | bytes 1966080 | tf_op jit(solution)/shard_map/all_gather | solution.py:10
  159.3 50.4 %all-gather.18.cloned.1.call-start = ((), (), s32[]{:S(2)}) async-start(), calls=%async_computation.7 | async-start | bytes 10616832 | tf_op jit(solution)/shard_map/all_gather | solution.py:27
  159.9 97.1 %all-gather.20.cloned.1.call-start = ((), (), s32[]{:S(2)}) async-start(), calls=%async_computation.8 | async-start | bytes 3538944 | tf_op jit(solution)/shard_map/all_gather | solution.py:67
  160.6 144.3 %reduce-scatter.5.cloned.1.call-start = ((), (), s32[]{:S(2)}) async-start(), calls=%async_computation.9 | async-start | bytes 3932160 | tf_op jit(solution)/shard_map/reduce_scatter | solution.py:70
  190.3 19.3 %copy-start.1 = (bf16[256,3072]{1,0:T(8,128)(2,1)S(1)}, bf16[256,3072]{1,0:T(8,128)(2,1)}, u32[]{:S(2)}) copy-start(bf16[256,3072]{1,0:T(8,128)(2,1)} %all-gather.16.cloned.1.call-done) | copy-start | bytes 4718596
  257.0 47.9 %copy-start.2 = (bf16[256,768]{1,0:T(8,128)(2,1)S(1)}, bf16[256,768]{1,0:T(8,128)(2,1)}, u32[]{:S(2)}) copy-start(bf16[256,768]{1,0:T(8,128)(2,1)} %add_convert_fusion.1) | copy-start | bytes 1179652
Sparse Core Ops, SparseCore 0:
  9.2 33.5 all-gather.9
  44.3 17.9 all-gather.11
  63.8 12.1 all-gather.13
  114.0 43.2 reduce-scatter.2
  159.4 30.8 all-gather.15
  191.7 17.9 all-gather.17
  211.2 12.1 all-gather.19
  261.6 43.2 reduce-scatter.4
where the time goes:
time: 314 us
  waiting for transfers between devices  172 us (55%)
  blocking collectives  88.5 us (28%)
  matrix products  22.8 us (7%)
  between operations  14.5 us (5%)
  other arithmetic  13.9 us (4%)
    reduce_scatter x2, waiting for transfers between devices, attend_block(): mine = lax.psum_scatter(projected, 'head', scatter_dimension=1, tiled=True)  86.7 us
    all_gather x2, waiting for transfers between devices, modulate(): whole = lax.all_gather(x_rows, 'head', axis=1, tiled=True)  50.1 us
    all_gather x2, blocking collectives, attend_block(): key_piece = lax.all_gather(key, 'seq', axis=0, tiled=True)  39.7 us
    all_gather x2, blocking collectives, attend_block(): value_piece = lax.all_gather(value, 'seq', axis=0, tiled=True)  36.2 us
    all_gather x2, waiting for transfers between devices, attend_block(): lax.all_gather(qkv_weight, 'branch', axis=0, tiled=True)  31.2 us
    all_gather x1, blocking collectives, attend_block(): keep_piece = lax.all_gather(keep_wire, 'seq', axis=0, tiled=True)  12.7 us
    dot_general x2, matrix products, attend_block(): jnp.einsum('rd,dsc->rsc', moded, lax.all_gather(qkv_weight, 'branch', axi...  10.5 us
    dot_general x2, matrix products, attend_block(): jnp.dot(attended, lax.all_gather(out_weight, 'branch', axis=1, tiled=True...  8.77 us
  transfers between devices with their start and end apart: 8, of which 6 were waited for; matrix products, arithmetic and copies ran while one was open for 8% of the time, Pallas kernels for 0%

commit v1 on v0

--- a/solution.py
+++ b/solution.py
@@ -7,7 +7,12 @@
 
 
 def modulate(x_rows, mod):
-    whole = lax.all_gather(x_rows, "head", axis=1, tiled=True)
+    ring = [x_rows]
+    for hop in range(3):
+        ring.append(lax.ppermute(ring[-1], "head", [(dev, (dev + 1) % 4) for dev in range(4)]))
+    whole = jnp.roll(
+        jnp.concatenate(ring[::-1], axis=1), (lax.axis_index("head") + 1) * ring[0].shape[1], axis=1
+    )
     xf = whole.astype(jnp.float32)
     mean = jnp.mean(xf, axis=1, keepdims=True)
     centered = xf - mean

time: 314 us -> 281 us (0.89)
  waiting for transfers between devices: 172 us -> 128 us
  starting transfers between devices: 0.28 us -> 8.31 us
  blocking collectives: 88.5 us -> 83 us
    all_gather x2 -> x0, waiting for transfers between devices: 50.1 us -> none  [modulate(): whole = lax.all_gather(x_rows, 'head', axis=1, tiled=True)]
    ppermute x0 -> x6, waiting for transfers between devices: none -> 43.4 us  [modulate(): lax.ppermute(ring[-1], 'head', [(dev, (dev + 1) % 4) for dev in range(4)])]
    all_gather x2, waiting for transfers between devices: 31.2 us -> 0.04 us  [attend_block(): lax.all_gather(qkv_weight, 'branch', axis=0, tiled=True)]
    ppermute x0 -> x6, starting transfers between devices: none -> 7.93 us  [modulate(): lax.ppermute(ring[-1], 'head', [(dev, (dev + 1) % 4) for dev in range(4)])]
    reduce_sum x2, other arithmetic: 3.63 us -> 9.78 us  [modulate(): mean = jnp.mean(xf, axis=1, keepdims=True)]
    reduce_scatter x2, waiting for transfers between devices: 86.7 us -> 83.5 us  [attend_block(): mine = lax.psum_scatter(projected, 'head', scatter_dimension=1, tiled=True)]
  transfers between devices with their start and end apart: 8 -> 12, of which waited for: 6 -> 7; matrix products, arithmetic and copies ran while one was open for 8% -> 13% of each run, Pallas kernels for 0% -> 0%
where the time goes in v1:
time: 281 us; the launch traced here: 280 us
  waiting for transfers between devices  128 us (46%)
  blocking collectives  83 us (30%)
  matrix products  24.1 us (9%)
  other arithmetic  17 us (6%)
  between operations  14.5 us (5%)
  starting transfers between devices  8.31 us (3%)
  local copies, waits for them, and re-layouts  5.24 us (2%)
    reduce_scatter x2, waiting for transfers between devices, attend_block(): mine = lax.psum_scatter(projected, 'head', scatter_dimension=1, tiled=True)  83.5 us
    ppermute x6, waiting for transfers between devices, modulate(): lax.ppermute(ring[-1], 'head', [(dev, (dev + 1) % 4) for dev in range(4)])  43.4 us
    all_gather x2, blocking collectives, attend_block(): key_piece = lax.all_gather(key, 'seq', axis=0, tiled=True)  37 us
    all_gather x2, blocking collectives, attend_block(): value_piece = lax.all_gather(value, 'seq', axis=0, tiled=True)  34.8 us
    all_gather x1, blocking collectives, attend_block(): keep_piece = lax.all_gather(keep_wire, 'seq', axis=0, tiled=True)  11.2 us
    dot_general x2, matrix products, attend_block(): jnp.einsum('rd,dsc->rsc', moded, lax.all_gather(qkv_weight, 'branch', axi...  10.6 us
    reduce_sum x2, other arithmetic, modulate(): mean = jnp.mean(xf, axis=1, keepdims=True)  9.78 us
    dot_general x2, matrix products, attend_block(): jnp.dot(attended, lax.all_gather(out_weight, 'branch', axis=1, tiled=True...  8.72 us
  transfers between devices with their start and end apart: 12, of which 7 were waited for; matrix products, arithmetic and copies ran while one was open for 13% of the time, Pallas kernels for 0%

profile of v1, /device:TPU:0, one launch (start us, length us, event | category | flops | bytes accessed | tf_op | source)
XLA Modules:
  0.0 280.4 jit_solution(10276680988238868127)
XLA Ops:
  7.5 3.0 %collective-permute-start = (bf16[256,768]{1,0:T(8,128)(2,1)S(1)}, bf16[256,768]{1,0:T(8,128)(2,1)S(1)}, u32[]{:S(2)}, u32[]{:S(2)}) collective-permute-start(bf16[256,768]{1,0:T(8,128)(2,1)S(1)} %copy-done), channel_id=1, source_target_pairs={{0,1},{1,2},{2,3},{3,0},{4,5},{5,6},{6,7},{7,4},{8,9},{9,10},{10,1... | collective-permute-start | bytes 1179656 | tf_op jit(solution)/shard_map/ppermute | solution.py:12
  11.3 11.2 %all-gather.2 = bf16[4,1,256]{2,1,0:T(2,128)(2,1)S(1)} all-gather(bf16[1,1,256]{2,1,0:T(2,128)(2,1)S(1)} %reshape.146), channel_id=1, replica_groups=mesh['branch'=2,'seq'=4,'head'=4] {'seq'}, dimensions={0}, use_global_device_ids=true | all-gather | bytes 2560 | tf_op jit(solution)/shard_map/all_gather | solution.py:50
  22.5 1.5 collective-permute-start.1
  24.7 7.3 %collective-permute-done.1 = bf16[256,768]{1,0:T(8,128)(2,1)S(1)} collective-permute-done((bf16[256,768]{1,0:T(8,128)(2,1)S(1)}, bf16[256,768]{1,0:T(8,128)(2,1)S(1)}, u32[]{:S(2)}, u32[]{:S(2)}) %collective-permute-start.1) | collective-permute-done | bytes 393248 | tf_op jit(solution)/shard_map/ppermute | solution.py:12
  33.9 6.8 %collective-permute-done.2 = bf16[256,768]{1,0:T(8,128)(2,1)S(1)} collective-permute-done((bf16[256,768]{1,0:T(8,128)(2,1)S(1)}, bf16[256,768]{1,0:T(8,128)(2,1)S(1)}, u32[]{:S(2)}, u32[]{:S(2)}) %collective-permute-start.2) | collective-permute-done | bytes 393248 | tf_op jit(solution)/shard_map/ppermute | solution.py:12
  40.7 4.9 %convert_reduce_fusion.1 = (f32[256]{0:T(256)S(1)}, bf16[256,3072]{1,0:T(8,128)(2,1)S(1)}) fusion(s32[]{:T(128)S(6)} %select_n.45, bf16[256,768]{1,0:T(8,128)(2,1)S(1)} %copy-done, bf16[256,768]{1,0:T(8,128)(2,1)S(1)} %collective-permute-done, bf16[256,768]{1,0:T(8,128)(2,1)S(1)} %collective-permute-done.1, bf16[256,768]{1,0:T(8,128)(2,1)S(1)} %collective-permute-done.2), kind=kLoop, calls=%fused_computation.3 | loop fusion | flops 14155520 | bytes 3146756 | tf_op jit(solution)/shard_map/reduce_sum | solution.py:17
  46.2 5.3 %fusion.33 = f32[256,3,384]{2,0,1:T(8,128)S(1)} fusion(bf16[3072,3,384]{2,0,1:T(8,128)(2,1)} %all-gather.8.cloned.1.call-done, bf16[256,3072]{1,0:T(8,128)(2,1)S(1)} %get-tuple-element.9, f32[3072]{0:T(1024)S(1)} %bitcast.90, f32[3072]{0:T(1024)S(1)} %bitcast.91, f32[256]{0:T(256)S(1)} %add_rsqrt_fusion.5, f32[256]{0:T(256)S(1)} %broadcast_multiply_fusion.1), kind=kOutput, calls=%fused_computation.57 | convolution fusion | flops 1816657920 | bytes 9857024 | tf_op jit(solution)/shard_map/rd,dsc->rsc/dot_general | solution.py:29
  52.0 19.1 %all_gather.30 = bf16[1024,384]{1,0:T(8,128)(2,1)S(1)} all-gather(bf16[256,384]{1,0:T(8,128)(2,1)S(1)} %fusion.75), channel_id=1, replica_groups=mesh['branch'=2,'seq'=4,'head'=4] {'seq'}, dimensions={0}, use_global_device_ids=true | all-gather | bytes 983040 | tf_op jit(solution)/shard_map/all_gather | solution.py:48
  71.6 17.4 %all-gather = bf16[1024,1,384]{2,0,1:T(8,128)(2,1)S(1)} all-gather(bf16[256,1,384]{2,0,1:T(8,128)(2,1)S(1)} %slice.109), channel_id=2, replica_groups=mesh['branch'=2,'seq'=4,'head'=4] {'seq'}, dimensions={0}, use_global_device_ids=true | all-gather | bytes 983040 | tf_op jit(solution)/shard_map/all_gather | solution.py:49
  89.3 1.5 fusion.12
  92.7 4.4 %fusion.96 = f32[256,3072]{1,0:T(8,128)} fusion(bf16[256,384]{0,1:T(8,128)(2,1)S(1)} %bitcast.87, bf16[384,3072]{1,0:T(8,128)(2,1)} %all-gather.10.cloned.1.call-done), kind=kOutput, calls=%fused_computation.136 | convolution fusion | flops 603979776 | bytes 5701632 | tf_op jit(solution)/shard_map/dot_general | solution.py:70
  98.4 41.0 %reduce-scatter.3.cloned.1.call-done = f32[256,768]{1,0:T(8,128)} async-done(((f32[256,3072]{1,0:T(8,128)}), f32[256,768]{1,0:T(8,128)}) %reduce-scatter.3.cloned.1.call-update) | async-done | bytes 786448 | tf_op jit(solution)/shard_map/reduce_scatter | solution.py:75
  140.6 1.5 collective-permute-start.3
  142.2 10.1 %collective-permute-done.3 = bf16[256,768]{1,0:T(8,128)(2,1)S(1)} collective-permute-done((bf16[256,768]{1,0:T(8,128)(2,1)S(1)}, bf16[256,768]{1,0:T(8,128)(2,1)S(1)}, u32[]{:S(2)}, u32[]{:S(2)}) %collective-permute-start.3) | collective-permute-done | bytes 393248 | tf_op jit(solution)/shard_map/ppermute | solution.py:12
  152.8 10.2 %collective-permute-done.4 = bf16[256,768]{1,0:T(8,128)(2,1)S(1)} collective-permute-done((bf16[256,768]{1,0:T(8,128)(2,1)S(1)}, bf16[256,768]{1,0:T(8,128)(2,1)S(1)}, u32[]{:S(2)}, u32[]{:S(2)}) %collective-permute-start.4) | collective-permute-done | bytes 393248 | tf_op jit(solution)/shard_map/ppermute | solution.py:12
  163.9 9.0 %collective-permute-done.5 = bf16[256,768]{1,0:T(8,128)(2,1)S(1)} collective-permute-done((bf16[256,768]{1,0:T(8,128)(2,1)S(1)}, bf16[256,768]{1,0:T(8,128)(2,1)S(1)}, u32[]{:S(2)}, u32[]{:S(2)}) %collective-permute-start.5) | collective-permute-done | bytes 393248 | tf_op jit(solution)/shard_map/ppermute | solution.py:12
  172.9 4.9 %convert_reduce_fusion = (f32[256]{0:T(256)S(1)}, bf16[256,3072]{1,0:T(8,128)(2,1)S(1)}) fusion(s32[]{:T(128)S(6)} %select_n.45, bf16[256,768]{1,0:T(8,128)(2,1)S(1)} %add_convert_fusion.1, bf16[256,768]{1,0:T(8,128)(2,1)S(1)} %collective-permute-done.3, bf16[256,768]{1,0:T(8,128)(2,1)S(1)} %collective-permute-done.4, ...), kind=kLoop, calls=%fused_computation.1 | loop fusion | flops 14155520 | bytes 3146756 | tf_op jit(solution)/shard_map/reduce_sum | solution.py:17
  178.4 5.3 %fusion.36 = f32[256,3,384]{2,0,1:T(8,128)S(1)} fusion(bf16[3072,3,384]{2,0,1:T(8,128)(2,1)} %all-gather.12.cloned.1.call-done, bf16[256,3072]{1,0:T(8,128)(2,1)S(1)} %get-tuple-element.7, f32[3072]{0:T(1024)} %bitcast.88, f32[3072]{0:T(1024)} %bitcast.89, f32[256]{0:T(256)S(1)} %add_rsqrt_fusion.4, f32[256]{0:T(256)S(1)} %broadcast_multiply_fusion), kind=kOutput, calls=%fused_computation.59 | convolution fusion | flops 1816657920 | bytes 9857024 | tf_op jit(solution)/shard_map/rd,dsc->rsc/dot_general | solution.py:29
  185.1 17.9 %all_gather.34 = bf16[1024,384]{1,0:T(8,128)(2,1)S(1)} all-gather(bf16[256,384]{1,0:T(8,128)(2,1)S(1)} %fusion.73), channel_id=1, replica_groups=mesh['branch'=2,'seq'=4,'head'=4] {'seq'}, dimensions={0}, use_global_device_ids=true | all-gather | bytes 983040 | tf_op jit(solution)/shard_map/all_gather | solution.py:48
  203.5 17.4 %all-gather.1 = bf16[1024,1,384]{2,0,1:T(8,128)(2,1)S(1)} all-gather(bf16[256,1,384]{2,0,1:T(8,128)(2,1)S(1)} %copy-done.1), channel_id=3, replica_groups=mesh['branch'=2,'seq'=4,'head'=4] {'seq'}, dimensions={0}, use_global_device_ids=true | all-gather | bytes 983040 | tf_op jit(solution)/shard_map/all_gather | solution.py:49
  221.3 1.4 fusion.13
  224.6 4.3 %fusion.97 = f32[256,3072]{1,0:T(8,128)} fusion(bf16[256,384]{0,1:T(8,128)(2,1)S(1)} %bitcast.86, bf16[384,3072]{1,0:T(8,128)(2,1)} %all-gather.14.cloned.1.call-done), kind=kOutput, calls=%fused_computation.137 | convolution fusion | flops 603979776 | bytes 5701632 | tf_op jit(solution)/shard_map/dot_general | solution.py:70
  229.0 42.5 %reduce-scatter.5.cloned.1.call-done = f32[256,768]{1,0:T(8,128)} async-done(((f32[256,3072]{1,0:T(8,128)}), f32[256,768]{1,0:T(8,128)}) %reduce-scatter.5.cloned.1.call-update) | async-done | bytes 786448 | tf_op jit(solution)/shard_map/reduce_scatter | solution.py:75
  271.5 2.0 fusion.71
  (81 shorter events, 16.0 us)
Async XLA Ops:
  6.5 1.0 copy-start
  6.5 17.5 %copy-start.2 = (f32[2,3,3072]{2,0,1:T(2,128)S(1)}, f32[2,3,3072]{2,0,1:T(2,128)}, u32[]{:S(2)}) copy-start(f32[2,3,3072]{2,0,1:T(2,128)} %param.16) | copy-start | bytes 221188
  6.5 26.8 %copy-start.4 = (f32[2,2,128]{2,1,0:T(2,128)S(1)}, f32[2,2,128]{2,1,0:T(2,128)}, u32[]{:S(2)}) copy-start(f32[2,2,128]{2,1,0:T(2,128)} %param.17) | copy-start | bytes 6148
  6.5 39.6 %all-gather.8.cloned.1.call-start = ((), (), s32[]{:S(2)}) async-start(), calls=%async_computation.2 | async-start | bytes 10616832 | tf_op jit(solution)/shard_map/all_gather | solution.py:32
  7.3 85.4 %all-gather.10.cloned.1.call-start = ((), (), s32[]{:S(2)}) async-start(), calls=%async_computation.3 | async-start | bytes 3538944 | tf_op jit(solution)/shard_map/all_gather | solution.py:72
  7.5 15.0 %collective-permute-start = (bf16[256,768]{1,0:T(8,128)(2,1)S(1)}, bf16[256,768]{1,0:T(8,128)(2,1)S(1)}, u32[]{:S(2)}, u32[]{:S(2)}) collective-permute-start(bf16[256,768]{1,0:T(8,128)(2,1)S(1)} %copy-done), channel_id=1, source_target_pairs={{0,1},{1,2},{2,3},{3,0},{4,5},{5,6},{6,7},{7,4},{8,9},{9,10},{10,1... | collective-permute-start | bytes 1179656 | tf_op jit(solution)/shard_map/ppermute | solution.py:12
  10.5 128.9 %reduce-scatter.3.cloned.1.call-start = ((), (), s32[]{:S(2)}) async-start(), calls=%async_computation.4 | async-start | bytes 3932160 | tf_op jit(solution)/shard_map/reduce_scatter | solution.py:75
  22.5 9.5 %collective-permute-start.1 = (bf16[256,768]{1,0:T(8,128)(2,1)S(1)}, bf16[256,768]{1,0:T(8,128)(2,1)S(1)}, u32[]{:S(2)}, u32[]{:S(2)}) collective-permute-start(bf16[256,768]{1,0:T(8,128)(2,1)S(1)} %collective-permute-done), channel_id=1, source_target_pairs={{0,1},{1,2},{2,3},{3,0},{4,5},{5,6},{6,7},{7,4},{8,9},{9,10},{10,1... | collective-permute-start | bytes 1179656 | tf_op jit(solution)/shard_map/ppermute | solution.py:12
  32.0 8.7 %collective-permute-start.2 = (bf16[256,768]{1,0:T(8,128)(2,1)S(1)}, bf16[256,768]{1,0:T(8,128)(2,1)S(1)}, u32[]{:S(2)}, u32[]{:S(2)}) collective-permute-start(bf16[256,768]{1,0:T(8,128)(2,1)S(1)} %collective-permute-done.1), channel_id=1, source_target_pairs={{0,1},{1,2},{2,3},{3,0},{4,5},{5,6},{6,7},{7,4},{8,9},{9,10},{10,1... | collective-permute-start | bytes 1179656 | tf_op jit(solution)/shard_map/ppermute | solution.py:12
  97.1 66.2 %copy-start.5 = (f32[128]{0:T(128)S(1)}, f32[128]{0:T(128)}, u32[]{:S(2)}) copy-start(f32[128]{0:T(128)} %get-tuple-element.23) | copy-start | bytes 1540
  97.1 81.3 %all-gather.12.cloned.1.call-start = ((), (), s32[]{:S(2)}) async-start(), calls=%async_computation.5 | async-start | bytes 10616832 | tf_op jit(solution)/shard_map/all_gather | solution.py:32
  97.7 126.9 %all-gather.14.cloned.1.call-start = ((), (), s32[]{:S(2)}) async-start(), calls=%async_computation.6 | async-start | bytes 3538944 | tf_op jit(solution)/shard_map/all_gather | solution.py:72
  140.6 11.6 %collective-permute-start.3 = (bf16[256,768]{1,0:T(8,128)(2,1)S(1)}, bf16[256,768]{1,0:T(8,128)(2,1)S(1)}, u32[]{:S(2)}, u32[]{:S(2)}) collective-permute-start(bf16[256,768]{1,0:T(8,128)(2,1)S(1)} %add_convert_fusion.1), channel_id=1, source_target_pairs={{0,1},{1,2},{2,3},{3,0},{4,5},{5,6},{6,7},{7,4},{8,9},{9,10},{10,1... | collective-permute-start | bytes 1179656 | tf_op jit(solution)/shard_map/ppermute | solution.py:12
  152.3 10.7 %collective-permute-start.4 = (bf16[256,768]{1,0:T(8,128)(2,1)S(1)}, bf16[256,768]{1,0:T(8,128)(2,1)S(1)}, u32[]{:S(2)}, u32[]{:S(2)}) collective-permute-start(bf16[256,768]{1,0:T(8,128)(2,1)S(1)} %collective-permute-done.3), channel_id=1, source_target_pairs={{0,1},{1,2},{2,3},{3,0},{4,5},{5,6},{6,7},{7,4},{8,9},{9,10},{10,1... | collective-permute-start | bytes 1179656 | tf_op jit(solution)/shard_map/ppermute | solution.py:12
  163.0 9.9 %collective-permute-start.5 = (bf16[256,768]{1,0:T(8,128)(2,1)S(1)}, bf16[256,768]{1,0:T(8,128)(2,1)S(1)}, u32[]{:S(2)}, u32[]{:S(2)}) collective-permute-start(bf16[256,768]{1,0:T(8,128)(2,1)S(1)} %collective-permute-done.4), channel_id=1, source_target_pairs={{0,1},{1,2},{2,3},{3,0},{4,5},{5,6},{6,7},{7,4},{8,9},{9,10},{10,1... | collective-permute-start | bytes 1179656 | tf_op jit(solution)/shard_map/ppermute | solution.py:12
  163.0 108.5 %reduce-scatter.5.cloned.1.call-start = ((), (), s32[]{:S(2)}) async-start(), calls=%async_computation.7 | async-start | bytes 3932160 | tf_op jit(solution)/shard_map/reduce_scatter | solution.py:75
  183.7 0.7 copy-start.3
  185.1 18.4 %copy-start.1 = (bf16[256,1,384]{2,0,1:T(8,128)(2,1)S(1)}, bf16[256,1,384]{2,0,1:T(8,128)(2,1)}, u32[]{:S(2)}) copy-start(bf16[256,1,384]{2,0,1:T(8,128)(2,1)} %slice.108) | copy-start | bytes 589828
Sparse Core Ops, SparseCore 0:
  8.9 20.6 all-gather.7
  31.1 12.1 all-gather.9
  97.2 42.1 reduce-scatter.2
  140.8 17.9 all-gather.11
  163.2 12.4 all-gather.13
  229.1 42.4 reduce-scatter.4
